TPU v7x, 128 devices: a whole 4x4x4 slice. The times are simulated.
128 devices in a mesh: band: 8 (over z_hi, y), lon: 16 (over z_lo, x, core).
Axes of the slice: x: 4, y: 4, z: 4 (z_hi: 2, z_lo: 2; z = z_hi * 2 + z_lo), core: 2. Of those that a mesh axis runs over, the one named last changes fastest.
Arguments:
- latent: bfloat16 [256, 2048, 256], P('band', 'lon'), may hold values from -6 to 6
- row_index: int32 [8, 16, 32], P('band', 'lon'), may hold values from 0 to 31
- interp_weights: bfloat16 [4096, 128, 128], P(('band', 'lon')), may hold values from -0.5 to 0.5
- observation_slot_index: int32 [4096, 128], P(('band', 'lon')), may hold values from 0 to 6
- counts: int32 [4096], P(('band', 'lon')), may hold values from 32 to 128
- targets: bfloat16 [4096, 128, 128], P(('band', 'lon')), may hold values from -6 to 6
- gain: float32 [256], replicated, may hold values from 0.5 to 1.5
- w_in: bfloat16 [256, 512], replicated, may hold values from -0.375 to 0.375
- w_out: bfloat16 [512, 256], replicated, may hold values from -0.25 to 0.25
- head: bfloat16 [256, 128], replicated, may hold values from -0.375 to 0.375
Outputs:
- grad_latent: float32 [256, 2048, 256], P('band', 'lon')
- grad_w_in: float32 [256, 512], replicated
- grad_w_out: float32 [512, 256], replicated
- grad_gain: float32 [256], replicated
- grad_head: float32 [256, 128], replicated
All inputs are finite; a program needn't handle non-finite values.
Results may differ from a plain program's by a relative error of at most 0.007.
Values may be sent and summed in bfloat16 or wider, within the bound.
No kernel may reach another device: no remote copies, remote signals or barrier semaphores. Data moves between devices by JAX's collectives and lax.ppermute only.
A program may use at most 128 MiB of HBM per device.

v0:
```python
import math
import jax
import jax.numpy as jnp
from jax import lax
from jax.sharding import PartitionSpec as P

WINDOW_SLOTS = 7
norm_eps = 1e-05


def padded_2(cells, sides, width):
    for axis, dim in sides:
        count = lax.axis_size(axis)
        head = lax.slice_in_dim(cells, 0, width, axis=dim)
        tail = lax.slice_in_dim(cells, cells.shape[dim] - width, cells.shape[dim], axis=dim)
        cells = jnp.concatenate(
            [
                lax.ppermute(tail, axis, [(i, (i + 1) % count) for i in range(count)]),
                cells,
                lax.ppermute(head, axis, [((i + 1) % count, i) for i in range(count)]),
            ],
            axis=dim,
        )
    return cells


def rounded_slots(values):
    return lax.optimization_barrier(values.astype(jnp.bfloat16))


def padded_mix(padded):
    return padded[:, 1:-1] + 0.5 * (padded[:, :-2] + padded[:, 2:])


def silu_slope(pre_act):
    sigmoid_a = jax.nn.sigmoid(pre_act)
    return sigmoid_a * (1.0 + pre_act * (1.0 - sigmoid_a))


def project_pair(weights, tile_pairs, temporal_weight, channels):
    proj_old = jnp.einsum(
        "bol,blc->boc", weights, tile_pairs[..., :channels], preferred_element_type=jnp.float32
    )
    proj_new = jnp.einsum(
        "bol,blc->boc", weights, tile_pairs[..., channels:], preferred_element_type=jnp.float32
    )
    return ((1.0 - temporal_weight) * proj_old + temporal_weight * proj_new).astype(jnp.bfloat16)


def pull_back(weights, obs_grad, temporal_weight):
    obs_float = obs_grad.astype(jnp.float32)
    back_old = ((1.0 - temporal_weight) * obs_float).astype(jnp.bfloat16)
    back_new = (temporal_weight * obs_float).astype(jnp.bfloat16)
    tile_old = jnp.einsum("bol,boc->blc", weights, back_old, preferred_element_type=jnp.float32)
    tile_new = jnp.einsum("bol,boc->blc", weights, back_new, preferred_element_type=jnp.float32)
    return jnp.concatenate([tile_old, tile_new], axis=-1).astype(jnp.bfloat16)


def decode(obs_latent, live_rows, goals, head, loss_scale):
    blocks, obs_rows, channels = obs_latent.shape
    flat_latent = obs_latent.reshape(-1, channels)
    predicted = jnp.dot(flat_latent, head, preferred_element_type=jnp.float32)
    residual = jnp.where(
        live_rows, predicted - goals.reshape(-1, head.shape[1]).astype(jnp.float32), 0.0
    )
    pred_grad = (residual * loss_scale).astype(jnp.bfloat16)
    head_grad = jnp.einsum("rc,rv->cv", flat_latent, pred_grad, preferred_element_type=jnp.float32)
    obs_grad = jnp.einsum("rv,cv->rc", pred_grad, head, preferred_element_type=jnp.float32).astype(
        jnp.bfloat16
    )
    return (head_grad, obs_grad.reshape(blocks, obs_rows, channels))


def body(
    latent,
    row_index,
    interp_weights,
    observation_slot_index,
    counts,
    targets,
    gain,
    w_in,
    w_out,
    head,
):
    lat_rows, lon_cells, channels = latent.shape
    peer_count = lax.axis_size("lon")
    devices_all = lax.axis_size("band") * peer_count
    blocks = interp_weights.shape[0]
    obs_rows = interp_weights.shape[1]
    per_peer = blocks // peer_count
    padded = padded_2(latent, (("lon", 1),), 1)
    summed = padded_mix(padded.astype(jnp.float32))
    inv_rms = lax.rsqrt(jnp.mean(summed * summed, axis=-1, keepdims=True) + norm_eps)
    normed = (summed * inv_rms * gain).astype(jnp.bfloat16)
    pre_act = jnp.einsum("lmc,ch->lmh", normed, w_in, preferred_element_type=jnp.float32)
    activated = jax.nn.silu(pre_act).astype(jnp.bfloat16)
    advanced = (
        latent.astype(jnp.float32)
        + jnp.einsum("lmh,hc->lmc", activated, w_out, preferred_element_type=jnp.float32)
    ).astype(jnp.bfloat16)
    stacked = jnp.concatenate([latent, advanced], axis=-1)
    requested = row_index.reshape(blocks)
    picked = stacked[requested]
    row_select = (requested[:, None] == jnp.arange(lat_rows, dtype=jnp.int32)[None, :]).astype(
        jnp.bfloat16
    )
    temporal_weight = rounded_slots(observation_slot_index.astype(jnp.float32) / (WINDOW_SLOTS - 1))
    live_flags = jnp.arange(obs_rows, dtype=jnp.int32)[None, :] < counts[:, None]
    live_rows = live_flags.reshape(-1, 1)
    loss_scale = 1.0 / math.sqrt(obs_rows)
    tile_pairs = lax.all_to_all(
        picked.reshape(peer_count, per_peer, lon_cells, 2 * channels),
        "lon",
        split_axis=0,
        concat_axis=0,
        tiled=True,
    )
    local_coef = temporal_weight.reshape(blocks, obs_rows, 1).astype(jnp.float32)
    obs_latent = project_pair(
        interp_weights, tile_pairs.reshape(blocks, lon_cells, 2 * channels), local_coef, channels
    )
    head_grad, obs_grad = decode(obs_latent, live_rows, targets, head, loss_scale)
    tile_grads = pull_back(interp_weights, obs_grad, local_coef)
    returned = lax.all_to_all(
        tile_grads.reshape(peer_count, per_peer, lon_cells, 2 * channels),
        "lon",
        split_axis=0,
        concat_axis=0,
        tiled=True,
    )
    grid_grad = jnp.einsum(
        "br,bx->rx",
        row_select,
        returned.reshape(blocks, lon_cells * 2 * channels),
        preferred_element_type=jnp.float32,
    )
    grid_grad = grid_grad.reshape(lat_rows, lon_cells, 2 * channels)
    grad_adv = grid_grad[..., channels:].astype(jnp.bfloat16)
    grad_out = jnp.einsum("lmh,lmc->hc", activated, grad_adv, preferred_element_type=jnp.float32)
    act_grad = jnp.einsum("lmc,hc->lmh", grad_adv, w_out, preferred_element_type=jnp.float32)
    pre_grad = (act_grad * silu_slope(pre_act)).astype(jnp.bfloat16)
    grad_in = jnp.einsum("lmc,lmh->ch", normed, pre_grad, preferred_element_type=jnp.float32)
    normed_grad = jnp.einsum("lmh,ch->lmc", pre_grad, w_in, preferred_element_type=jnp.float32)
    grad_gain = jnp.sum(normed_grad * summed * inv_rms, axis=(0, 1))
    gained = normed_grad * gain
    summed_grad = inv_rms * (
        gained - summed * inv_rms * inv_rms * jnp.mean(gained * summed, axis=-1, keepdims=True)
    )
    grad_padded = padded_2(summed_grad.astype(jnp.bfloat16), (("lon", 1),), 1).astype(
        summed_grad.dtype
    )
    grad_latent = grid_grad[..., :channels] + grid_grad[..., channels:] + padded_mix(grad_padded)
    totals = lax.psum((grad_in, grad_out, grad_gain, head_grad), ("band", "lon"))
    return (
        grad_latent,
        totals[0] / devices_all,
        totals[1] / devices_all,
        totals[2] / devices_all,
        totals[3] / devices_all,
    )


def solution(mesh):
    return jax.shard_map(
        body,
        mesh=mesh,
        in_specs=(
            P("band", "lon", None),
            P("band", "lon", None),
            P(("band", "lon"), None, None),
            P(("band", "lon"), None),
            P(("band", "lon")),
            P(("band", "lon"), None, None),
            P(),
            P(),
            P(),
            P(),
        ),
        out_specs=(P("band", "lon", None), P(), P(), P(), P()),
        check_vma=False,
    )
```

profile of v0, /device:TPU:1, one launch (start us, length us, event | category | flops | bytes accessed | tf_op | source)
XLA Modules:
  0.0 456.2 jit_solution(16606701495915434797)
XLA Ops:
  7.2 2.9 copy.28
  10.1 2.7 collective-permute-start
  12.8 0.8 collective-permute-done
  13.6 2.6 collective-permute-done.1
  16.5 0.8 multiply_reduce_fusion.2
  17.4 0.8 multiply_convert_fusion.5
  18.5 5.2 %multiply_convert_fusion.1 = (bf16[32,128,512]{2,1,0:T(8,128)(2,1)S(1)}, f32[32,128,512]{2,1,0:T(8,128)}) fusion(bf16[256,512]{1,0:T(8,128)(2,1)S(1)} %copy-done.21, bf16[32,128,256]{2,0,1:T(8,128)(2,1)S(1)} %multiply_convert_fusion.5), kind=kOutput, calls=%fused_computation.2 | convolution fusion | flops 1084227584 | bytes 14942208 | tf_op jit(solution)/shard_map/lmc,ch->lmh/dot_general | solution.py:96
  23.7 1.9 copy-done.10
  25.6 1.3 add_convert_fusion.1
  26.9 2.3 pad_maximum_fusion
  29.2 5.0 %gather_fusion = bf16[32,128,512]{2,1,0:T(8,128)(2,1)} fusion(bf16[32,128,512]{2,1,0:T(8,128)(2,1)} %pad_maximum_fusion, s32[1024]{0:T(1024)S(1)} %pad_clamp_fusion), kind=kCustom, calls=%fused_computation | custom fusion | bytes 8388736 | tf_op jit(solution)/shard_map/gather | solution.py:104
  34.2 6.4 %all-to-all-start = ((bf16[16,2,128,512]{3,2,1,0:T(8,128)(2,1)}), bf16[16,2,128,512]{3,2,1,0:T(8,128)(2,1)}, u32[]{:S(2)}, u32[]{:S(2)}) async-start(bf16[16,2,128,512]{3,2,1,0:T(8,128)(2,1)} %bitcast.68), calls=%async_computation | async-start | bytes 8388608 | tf_op jit(solution)/shard_map/all_to_all | solution.py:112
  40.8 56.3 %all-to-all-done = bf16[16,2,128,512]{3,2,1,0:T(8,128)(2,1)} async-done(((bf16[16,2,128,512]{3,2,1,0:T(8,128)(2,1)}), bf16[16,2,128,512]{3,2,1,0:T(8,128)(2,1)}, u32[]{:S(2)}, u32[]{:S(2)}) %all-to-all-start) | async-done | bytes 4194336 | tf_op jit(solution)/shard_map/all_to_all | solution.py:112
  97.0 2.3 fusion.18
  99.4 2.6 add_convert_fusion
  102.0 1.4 copy-done.6
  103.4 2.3 fusion.2
  105.7 1.1 copy-done.8
  106.7 0.7 convolution_convert_fusion
  107.4 3.4 copy.32
  110.9 3.0 fusion.24
  113.9 0.4 copy-done.3
  114.3 2.0 fusion.25
  116.3 3.9 copy.34
  120.3 2.6 copy.35
  122.8 4.6 %pad_maximum_fusion.1 = bf16[16,2,128,512]{3,2,1,0:T(8,128)(2,1)} fusion(bf16[16,2,128,256]{3,2,1,0:T(8,128)(2,1)} %copy.35, bf16[16,2,128,256]{3,2,1,0:T(8,128)(2,1)} %copy.34), kind=kLoop, calls=%fused_computation.21 | loop fusion | flops 8388608 | bytes 8388608 | tf_op jit(solution)/shard_map/concatenate | solution.py:56
  127.5 5.1 %all-to-all-start.1 = ((bf16[16,2,128,512]{3,2,1,0:T(8,128)(2,1)}), bf16[16,2,128,512]{3,2,1,0:T(8,128)(2,1)}, u32[]{:S(2)}, u32[]{:S(2)}) async-start(bf16[16,2,128,512]{3,2,1,0:T(8,128)(2,1)} %pad_maximum_fusion.1), calls=%async_computation.1 | async-start | bytes 8388608 | tf_op jit(solution)/shard_map/all_to_all | solution.py:125
  132.9 1.4 fusion.47
  134.3 54.1 %all-to-all-done.1 = bf16[16,2,128,512]{3,2,1,0:T(8,128)(2,1)} async-done(((bf16[16,2,128,512]{3,2,1,0:T(8,128)(2,1)}), bf16[16,2,128,512]{3,2,1,0:T(8,128)(2,1)}, u32[]{:S(2)}, u32[]{:S(2)}) %all-to-all-start.1) | async-done | bytes 4194336 | tf_op jit(solution)/shard_map/all_to_all | solution.py:125
  188.4 5.4 %fusion.3 = f32[32,128,512]{2,0,1:T(8,128)S(1)} fusion(s32[32]{0:T(128)S(1)} %bitcast.74, bf16[4,8,128,512]{3,2,1,0:T(8,128)(2,1)} %bitcast.28), kind=kOutput, calls=%fused_computation.9 | convolution fusion | flops 134218752 | bytes 12583040 | tf_op jit(solution)/shard_map/br,bx->rx/dot_general | solution.py:132
  194.2 4.9 %copy-done.11 = bf16[32,128,512]{2,1,0:T(8,128)(2,1)S(1)} copy-done((bf16[32,128,512]{2,1,0:T(8,128)(2,1)S(1)}, bf16[32,128,512]{2,1,0:T(8,128)(2,1)}, u32[]{:S(2)}) %copy-start.11) | copy-done | bytes 4194328
  199.1 3.6 fusion.32
  202.6 6.6 %multiply_convert_fusion = bf16[32,128,512]{2,1,0:T(8,128)(2,1)S(1)} fusion(f32[32,128,512]{2,1,0:T(8,128)} %get-tuple-element.27, bf16[32,128,256]{2,0,1:T(8,128)(2,1)S(1)} %slice.98, bf16[512,256]{1,0:T(8,128)(2,1)S(1)} %copy-done.14), kind=kOutput, calls=%fused_computation.1 | convolution fusion | flops 1092616192 | bytes 14942208 | tf_op jit(solution)/shard_map/lmc,hc->lmh/dot_general | solution.py:141
  209.2 1.9 copy-done.23
  211.2 3.7 fusion.29
  214.8 8.9 %multiply_reduce_fusion = (f32[256]{0:T(256)S(1)}, f32[32,128]{0,1:T(8,128)S(1)}, f32[32,128,256]{2,0,1:T(8,128)}) fusion(f32[32,128,256]{2,0,1:T(8,128)} %copy-done.4, f32[32,128]{0,1:T(8,128)S(1)} %add_rsqrt_fusion, f32[256]{0:T(256)S(1)} %copy-done.17, bf16[256,512]{1,0:T(8,128)(2,1)S(1)} %copy-done.22, bf16[32,128,512]{2,1,0:T(8,128)(2,1)} %copy-done.23), kind=kOutput, calls=%fused_computation.22 | convolution fusion | flops 1080028928 | bytes 12879872 | tf_op jit(solution)/shard_map/lmh,ch->lmc/dot_general | solution.py:144
  223.7 67.3 %psum.30 = f32[256]{0:T(256)S(1)} all-reduce(f32[256]{0:T(256)S(1)} %get-tuple-element.15), channel_id=1, replica_groups=mesh['band'=8,'lon'=16] {'band','lon'}, use_global_device_ids=true, to_apply=%region_5.6 | all-reduce | flops 256 | bytes 2048 | tf_op jit(solution)/shard_map/psum | solution.py:154
  291.1 4.1 multiply_convert_fusion.2
  295.2 0.7 collective-permute-start.2
  295.9 0.5 collective-permute-start.3
  296.4 0.6 broadcast_multiply_fusion.4
  297.0 2.0 collective-permute-done.3
  299.4 5.1 %fusion.8 = f32[32,128,256]{2,0,1:T(8,128)S(1)} fusion(f32[32,130,256]{2,0,1:T(8,128)S(1)} %maximum_convert_fusion.1, f32[32,128,512]{2,0,1:T(8,128)} %copy-done.2), kind=kLoop, calls=%fused_computation.15 | loop fusion | flops 5242880 | bytes 25165824 | tf_op jit(solution)/shard_map/add | solution.py:153
  304.5 4.4 copy.43
  309.0 135.1 %all-reduce.3.cloned.1.call-done = (f32[256,512]{1,0:T(8,128)}, f32[512,256]{1,0:T(8,128)}, f32[256,128]{1,0:T(8,128)}) async-done(((f32[256,512]{1,0:T(8,128)}, f32[512,256]{1,0:T(8,128)}, f32[256,128]{1,0:T(8,128)}), (f32[256,512]{1,0:T(8,128)}, f32[512,256]{1,0:T(8,128)}, f32[256,128]{1,0:T(8,128)})) %all-reduce.3.cloned.1.call-update) | async-done | bytes 1179664 | tf_op jit(solution)/shard_map/psum | solution.py:154
  444.1 1.9 broadcast_multiply_fusion.1
  445.9 1.6 broadcast_multiply_fusion.2
  447.5 1.9 broadcast_multiply_fusion
  (59 shorter events, 1.8 us)
Async XLA Ops:
  7.2 89.9 %copy-start = (bf16[32,128,128]{2,1,0:T(8,128)(2,1)S(1)}, bf16[32,128,128]{2,1,0:T(8,128)(2,1)}, u32[]{:S(2)}) copy-start(bf16[32,128,128]{2,1,0:T(8,128)(2,1)} %param.12) | copy-start | bytes 3145732
  7.2 5.6 %copy-start.18 = (s32[1,1,32]{2,1,0:T(1,128)S(1)}, s32[1,1,32]{2,1,0:T(1,128)}, u32[]{:S(2)}) copy-start(s32[1,1,32]{2,1,0:T(1,128)} %param.11) | copy-start | bytes 388
  10.1 3.5 collective-permute-start
  12.7 3.5 collective-permute-start.1
  16.5 0.9 copy-start.17
  17.4 6.3 %copy-start.4 = (f32[32,128,256]{2,0,1:T(8,128)}, f32[32,128,256]{2,0,1:T(8,128)S(1)}, u32[]{:S(2)}) copy-start(f32[32,128,256]{2,0,1:T(8,128)S(1)} %get-tuple-element.21) | copy-start | bytes 12582916
  17.4 1.1 copy-start.21
  18.5 5.2 %copy-start.12 = (bf16[32,128,256]{2,0,1:T(8,128)(2,1)}, bf16[32,128,256]{2,0,1:T(8,128)(2,1)S(1)}, u32[]{:S(2)}) copy-start(bf16[32,128,256]{2,0,1:T(8,128)(2,1)S(1)} %multiply_convert_fusion.5) | copy-start | bytes 6291460
  18.5 7.1 %copy-start.5 = (bf16[32,128,256]{2,1,0:T(8,128)(2,1)S(1)}, bf16[32,128,256]{2,1,0:T(8,128)(2,1)}, u32[]{:S(2)}) copy-start(bf16[32,128,256]{2,1,0:T(8,128)(2,1)} %param.10) | copy-start | bytes 6291460
  18.5 7.1 %copy-start.14 = (bf16[512,256]{1,0:T(8,128)(2,1)S(1)}, bf16[512,256]{1,0:T(8,128)(2,1)}, u32[]{:S(2)}) copy-start(bf16[512,256]{1,0:T(8,128)(2,1)} %param.18) | copy-start | bytes 786436
  23.7 1.9 copy-start.10
  34.2 6.5 %copy-start.16 = (s32[32,128]{1,0:T(8,128)S(1)}, s32[32,128]{1,0:T(8,128)}, u32[]{:S(2)}) copy-start(s32[32,128]{1,0:T(8,128)} %param.13) | copy-start | bytes 49156
  34.2 6.5 %copy-start.19 = (s32[32]{0:T(128)S(1)}, s32[32]{0:T(128)}, u32[]{:S(2)}) copy-start(s32[32]{0:T(128)} %param.14) | copy-start | bytes 388
  34.2 62.8 %all-to-all-start = ((bf16[16,2,128,512]{3,2,1,0:T(8,128)(2,1)}), bf16[16,2,128,512]{3,2,1,0:T(8,128)(2,1)}, u32[]{:S(2)}, u32[]{:S(2)}) async-start(bf16[16,2,128,512]{3,2,1,0:T(8,128)(2,1)} %bitcast.68), calls=%async_computation | async-start | bytes 8388608 | tf_op jit(solution)/shard_map/all_to_all | solution.py:112
  99.3 4.1 copy-start.15
  99.3 4.1 copy-start.20
  102.0 1.4 copy-start.6
  105.7 1.1 copy-start.8
  110.9 3.4 copy-start.3
  127.5 5.4 %copy-start.7 = (bf16[32,256,128]{1,2,0:T(8,128)(2,1)S(1)}, bf16[32,256,128]{1,2,0:T(8,128)(2,1)}, u32[]{:S(2)}) copy-start(bf16[32,256,128]{1,2,0:T(8,128)(2,1)} %copy-done.6) | copy-start | bytes 6291460
  127.5 5.4 %copy-start.9 = (bf16[4096,128]{1,0:T(8,128)(2,1)S(1)}, bf16[4096,128]{1,0:T(8,128)(2,1)}, u32[]{:S(2)}) copy-start(bf16[4096,128]{1,0:T(8,128)(2,1)} %copy-done.8) | copy-start | bytes 3145732
  127.5 60.9 %all-to-all-start.1 = ((bf16[16,2,128,512]{3,2,1,0:T(8,128)(2,1)}), bf16[16,2,128,512]{3,2,1,0:T(8,128)(2,1)}, u32[]{:S(2)}, u32[]{:S(2)}) async-start(bf16[16,2,128,512]{3,2,1,0:T(8,128)(2,1)} %pad_maximum_fusion.1), calls=%async_computation.1 | async-start | bytes 8388608 | tf_op jit(solution)/shard_map/all_to_all | solution.py:125
  132.6 311.5 %all-reduce.3.cloned.1.call-start = ((), (), s32[]{:S(2)}) async-start(), calls=%async_computation.2 | async-start | bytes 2359296 | tf_op jit(solution)/shard_map/psum | solution.py:154
  193.8 8.8 %copy-start.2 = (f32[32,128,512]{2,0,1:T(8,128)}, f32[32,128,512]{2,0,1:T(8,128)S(1)}, u32[]{:S(2)}) copy-start(f32[32,128,512]{2,0,1:T(8,128)S(1)} %fusion.3) | copy-start | bytes 25165828
  193.8 5.2 %copy-start.11 = (bf16[32,128,512]{2,1,0:T(8,128)(2,1)S(1)}, bf16[32,128,512]{2,1,0:T(8,128)(2,1)}, u32[]{:S(2)}) copy-start(bf16[32,128,512]{2,1,0:T(8,128)(2,1)} %copy-done.10) | copy-start | bytes 12582916
  202.6 8.5 %copy-start.13 = (bf16[32,128,256]{2,0,1:T(8,128)(2,1)S(1)}, bf16[32,128,256]{2,0,1:T(8,128)(2,1)}, u32[]{:S(2)}) copy-start(bf16[32,128,256]{2,0,1:T(8,128)(2,1)} %copy-done.12) | copy-start | bytes 6291460
  209.2 2.0 copy-start.23
  211.1 3.7 copy-start.22
  295.2 1.8 collective-permute-start.2
  295.9 3.2 collective-permute-start.3
  299.4 150.0 %copy-start.1 = (bf16[32,128,128]{2,1,0:T(8,128)(2,1)S(1)}, bf16[32,128,128]{2,1,0:T(8,128)(2,1)}, u32[]{:S(2)}) copy-start(bf16[32,128,128]{2,1,0:T(8,128)(2,1)} %param.12) | copy-start | bytes 3145732
Sparse Core Ops, SparseCore 0:
  297.2 146.8 all-reduce.2
where the time goes:
time: 457 us; the launch traced here: 456 us
  waiting for transfers between devices  251 us (55%)
  blocking collectives  67.3 us (15%)
  matrix products  48.9 us (11%)
  local copies, waits for them, and re-layouts  34.6 us (8%)
  other arithmetic  24.4 us (5%)
  starting transfers between devices  15.7 us (3%)
  between operations  14.3 us (3%)
    psum x1, waiting for transfers between devices, body(): lax.psum((grad_in, grad_out, grad_gain, head_grad), ('band', 'lon'))  135 us
    psum x1, blocking collectives, body(): lax.psum((grad_in, grad_out, grad_gain, head_grad), ('band', 'lon'))  67.3 us
    all_to_all x1, waiting for transfers between devices, body(): lax.all_to_all(picked.reshape(peer_count, per_peer, lon_cells, 2 * channe...  56.3 us
    all_to_all x1, waiting for transfers between devices, body(): lax.all_to_all(tile_grads.reshape(peer_count, per_peer, lon_cells, 2 * ch...  54.1 us
    unnamed x50, local copies, waits for them, and re-layouts  19.3 us
  transfers between devices with their start and end apart: 7, of which 6 were waited for; matrix products, arithmetic and copies ran while one was open for 3% of the time, Pallas kernels for 0%

commit v1 on v0

--- a/solution.py
+++ b/solution.py
@@ -6,6 +6,11 @@
 
 WINDOW_SLOTS = 7
 norm_eps = 1e-05
+
+
+def by_each_axis(value, inner_axis, outer_axis):
+    inner = lax.psum(value, inner_axis)
+    return lax.psum(inner, outer_axis)
 
 
 def padded_2(cells, sides, width):
@@ -151,7 +156,7 @@
         summed_grad.dtype
     )
     grad_latent = grid_grad[..., :channels] + grid_grad[..., channels:] + padded_mix(grad_padded)
-    totals = lax.psum((grad_in, grad_out, grad_gain, head_grad), ("band", "lon"))
+    totals = by_each_axis((grad_in, grad_out, grad_gain, head_grad), "band", "lon")
     return (
         grad_latent,
         totals[0] / devices_all,

time: 457 us -> 439 us (0.961)
  blocking collectives: 67.3 us -> 50 us
  starting transfers between devices: 15.7 us -> 21.4 us
    psum x1 -> x2, blocking collectives: 67.3 us -> 50 us  [the longest x1 33 us: by_each_axis(): return lax.psum(inner, outer_axis)]
    ppermute x2, starting transfers between devices: 3.36 us -> 9.31 us  [padded_2(): lax.ppermute(tail, axis, [(i, (i + 1) % count) for i in range(count)])]
    psum x1 -> x2, waiting for transfers between devices: 135 us -> 135 us  [the longest x1 76 us: by_each_axis(): inner = lax.psum(value, inner_axis)]
    unnamed x50 -> x52, local copies, waits for them, and re-layouts: 19.3 us -> 19.3 us
  transfers between devices with their start and end apart: 7 -> 8, of which waited for: 6 -> 6; matrix products, arithmetic and copies ran while one was open for 3% -> 5% of each run, Pallas kernels for 0% -> 0%
where the time goes in v1:
time: 439 us; the launch traced here: 438 us
  waiting for transfers between devices  249 us (57%)
  blocking collectives  50 us (11%)
  matrix products  47.2 us (11%)
  local copies, waits for them, and re-layouts  34.6 us (8%)
  other arithmetic  21.7 us (5%)
  starting transfers between devices  21.4 us (5%)
  between operations  14.4 us (3%)
    psum x1, waiting for transfers between devices, by_each_axis(): inner = lax.psum(value, inner_axis)  76 us
    psum x1, waiting for transfers between devices, by_each_axis(): return lax.psum(inner, outer_axis)  59 us
    all_to_all x1, waiting for transfers between devices, body(): lax.all_to_all(picked.reshape(peer_count, per_peer, lon_cells, 2 * channe...  56.3 us
    all_to_all x1, waiting for transfers between devices, body(): lax.all_to_all(tile_grads.reshape(peer_count, per_peer, lon_cells, 2 * ch...  54.1 us
    psum x1, blocking collectives, by_each_axis(): return lax.psum(inner, outer_axis)  33 us
    unnamed x52, local copies, waits for them, and re-layouts  19.3 us
    psum x1, blocking collectives, by_each_axis(): inner = lax.psum(value, inner_axis)  17 us
    ppermute x2, starting transfers between devices, padded_2(): lax.ppermute(tail, axis, [(i, (i + 1) % count) for i in range(count)])  9.31 us
  transfers between devices with their start and end apart: 8, of which 6 were waited for; matrix products, arithmetic and copies ran while one was open for 5% of the time, Pallas kernels for 0%

profile of v1, /device:TPU:1, one launch (start us, length us, event | category | flops | bytes accessed | tf_op | source)
XLA Modules:
  0.0 438.2 jit_solution(5191102673704235029)
XLA Ops:
  7.2 2.9 copy.28
  10.1 2.7 collective-permute-start
  12.8 0.8 collective-permute-done
  13.6 2.6 collective-permute-done.1
  16.5 0.8 multiply_reduce_fusion.2
  17.4 0.8 multiply_convert_fusion.5
  18.5 5.2 %multiply_convert_fusion.1 = (bf16[32,128,512]{2,1,0:T(8,128)(2,1)S(1)}, f32[32,128,512]{2,1,0:T(8,128)}) fusion(bf16[256,512]{1,0:T(8,128)(2,1)S(1)} %copy-done.22, bf16[32,128,256]{2,0,1:T(8,128)(2,1)S(1)} %multiply_convert_fusion.5), kind=kOutput, calls=%fused_computation.2 | convolution fusion | flops 1084227584 | bytes 14942208 | tf_op jit(solution)/shard_map/lmc,ch->lmh/dot_general | solution.py:101
  23.7 1.9 copy-done.11
  25.6 1.3 add_convert_fusion.1
  26.9 2.3 pad_maximum_fusion
  29.2 5.0 %gather_fusion = bf16[32,128,512]{2,1,0:T(8,128)(2,1)} fusion(bf16[32,128,512]{2,1,0:T(8,128)(2,1)} %pad_maximum_fusion, s32[1024]{0:T(1024)S(1)} %pad_clamp_fusion), kind=kCustom, calls=%fused_computation | custom fusion | bytes 8388736 | tf_op jit(solution)/shard_map/gather | solution.py:109
  34.2 6.4 %all-to-all-start = ((bf16[16,2,128,512]{3,2,1,0:T(8,128)(2,1)}), bf16[16,2,128,512]{3,2,1,0:T(8,128)(2,1)}, u32[]{:S(2)}, u32[]{:S(2)}) async-start(bf16[16,2,128,512]{3,2,1,0:T(8,128)(2,1)} %bitcast.68), calls=%async_computation | async-start | bytes 8388608 | tf_op jit(solution)/shard_map/all_to_all | solution.py:117
  40.8 56.3 %all-to-all-done = bf16[16,2,128,512]{3,2,1,0:T(8,128)(2,1)} async-done(((bf16[16,2,128,512]{3,2,1,0:T(8,128)(2,1)}), bf16[16,2,128,512]{3,2,1,0:T(8,128)(2,1)}, u32[]{:S(2)}, u32[]{:S(2)}) %all-to-all-start) | async-done | bytes 4194336 | tf_op jit(solution)/shard_map/all_to_all | solution.py:117
  97.0 2.3 fusion.18
  99.4 2.6 add_convert_fusion
  102.0 1.4 copy-done.7
  103.4 2.3 fusion.2
  105.7 1.1 copy-done.9
  106.7 0.7 convolution_convert_fusion
  107.4 3.4 copy.32
  110.9 3.0 fusion.24
  113.9 0.4 copy-done.3
  114.3 2.0 fusion.25
  116.3 3.9 copy.34
  120.3 2.6 copy.35
  122.8 4.6 %pad_maximum_fusion.1 = bf16[16,2,128,512]{3,2,1,0:T(8,128)(2,1)} fusion(bf16[16,2,128,256]{3,2,1,0:T(8,128)(2,1)} %copy.35, bf16[16,2,128,256]{3,2,1,0:T(8,128)(2,1)} %copy.34), kind=kLoop, calls=%fused_computation.21 | loop fusion | flops 8388608 | bytes 8388608 | tf_op jit(solution)/shard_map/concatenate | solution.py:61
  127.5 5.1 %all-to-all-start.1 = ((bf16[16,2,128,512]{3,2,1,0:T(8,128)(2,1)}), bf16[16,2,128,512]{3,2,1,0:T(8,128)(2,1)}, u32[]{:S(2)}, u32[]{:S(2)}) async-start(bf16[16,2,128,512]{3,2,1,0:T(8,128)(2,1)} %pad_maximum_fusion.1), calls=%async_computation.1 | async-start | bytes 8388608 | tf_op jit(solution)/shard_map/all_to_all | solution.py:130
  132.9 1.4 fusion.47
  134.3 54.1 %all-to-all-done.1 = bf16[16,2,128,512]{3,2,1,0:T(8,128)(2,1)} async-done(((bf16[16,2,128,512]{3,2,1,0:T(8,128)(2,1)}), bf16[16,2,128,512]{3,2,1,0:T(8,128)(2,1)}, u32[]{:S(2)}, u32[]{:S(2)}) %all-to-all-start.1) | async-done | bytes 4194336 | tf_op jit(solution)/shard_map/all_to_all | solution.py:130
  188.4 5.4 %fusion.3 = f32[32,128,512]{2,0,1:T(8,128)S(1)} fusion(s32[32]{0:T(128)S(1)} %bitcast.74, bf16[4,8,128,512]{3,2,1,0:T(8,128)(2,1)} %bitcast.28), kind=kOutput, calls=%fused_computation.9 | convolution fusion | flops 134218752 | bytes 12583040 | tf_op jit(solution)/shard_map/br,bx->rx/dot_general | solution.py:137
  194.2 4.9 %copy-done.12 = bf16[32,128,512]{2,1,0:T(8,128)(2,1)S(1)} copy-done((bf16[32,128,512]{2,1,0:T(8,128)(2,1)S(1)}, bf16[32,128,512]{2,1,0:T(8,128)(2,1)}, u32[]{:S(2)}) %copy-start.12) | copy-done | bytes 4194328
  199.1 3.6 fusion.32
  202.6 6.6 %multiply_convert_fusion = bf16[32,128,512]{2,1,0:T(8,128)(2,1)S(1)} fusion(f32[32,128,512]{2,1,0:T(8,128)} %get-tuple-element.30, bf16[32,128,256]{2,0,1:T(8,128)(2,1)S(1)} %slice.98, bf16[512,256]{1,0:T(8,128)(2,1)S(1)} %copy-done.15), kind=kOutput, calls=%fused_computation.1 | convolution fusion | flops 1092616192 | bytes 14942208 | tf_op jit(solution)/shard_map/lmc,hc->lmh/dot_general | solution.py:146
  209.2 1.9 copy-done.24
  211.2 3.7 fusion.29
  215.2 7.2 %multiply_reduce_fusion = (f32[256]{0:T(256)S(1)}, f32[32,128]{0,1:T(8,128)S(1)}, f32[32,128,256]{2,0,1:T(8,128)S(1)}) fusion(f32[32,128,256]{2,0,1:T(8,128)} %copy-done.4, f32[32,128]{0,1:T(8,128)S(1)} %add_rsqrt_fusion, f32[256]{0:T(256)S(1)} %copy-done.18, bf16[256,512]{1,0:T(8,128)(2,1)S(1)} %copy-done.23, bf16[32,128,512]{2,1,0:T(8,128)(2,1)} %copy-done.24), kind=kOutput, calls=%fused_computation.22 | convolution fusion | flops 1080028928 | bytes 12879872 | tf_op jit(solution)/shard_map/lmh,ch->lmc/dot_general | solution.py:149
  222.4 1.6 multiply_convert_fusion.2
  224.1 76.0 %all-reduce.7.cloned.1.call-done = (f32[256,512]{1,0:T(8,128)}, f32[512,256]{1,0:T(8,128)}, f32[256,128]{1,0:T(8,128)}) async-done(((f32[256,512]{1,0:T(8,128)}, f32[512,256]{1,0:T(8,128)}, f32[256,128]{1,0:T(8,128)}), (f32[256,512]{1,0:T(8,128)}, f32[512,256]{1,0:T(8,128)}, f32[256,128]{1,0:T(8,128)})) %all-reduce.7.cloned.1.call-update) | async-done | bytes 1179664 | tf_op jit(solution)/shard_map/psum | solution.py:12
  300.1 6.6 %collective-permute-start.2 = (bf16[32,1,256]{2,0,1:T(8,128)(2,1)S(1)}, bf16[32,1,256]{2,0,1:T(8,128)(2,1)S(1)}, u32[]{:S(2)}, u32[]{:S(2)}) collective-permute-start(bf16[32,1,256]{2,0,1:T(8,128)(2,1)S(1)} %get-tuple-element.25), channel_id=1, source_target_pairs={{0,1},{1,2},{2,3},{3,4},{4,5},{5,6},{6,7},{7,8},{8,9},{9,10},{10,1... | collective-permute-start | bytes 49160 | tf_op jit(solution)/shard_map/ppermute | solution.py:23
  306.8 17.0 %psum.60 = f32[256]{0:T(256)S(1)} all-reduce(f32[256]{0:T(256)S(1)} %get-tuple-element.15), channel_id=1, replica_groups=mesh['band'=8,'lon'=16] {'band'}, use_global_device_ids=true, to_apply=%region_7.8 | all-reduce | flops 256 | bytes 2048 | tf_op jit(solution)/shard_map/psum | solution.py:12
  323.8 33.0 %psum.61 = f32[256]{0:T(256)S(1)} all-reduce(f32[256]{0:T(256)S(1)} %psum.60), channel_id=1, replica_groups=mesh['band'=8,'lon'=16] {'lon'}, use_global_device_ids=true, to_apply=%region_8.9 | all-reduce | flops 256 | bytes 2048 | tf_op jit(solution)/shard_map/psum | solution.py:13
  356.8 0.6 broadcast_multiply_fusion.4
  357.7 4.9 %fusion.8 = f32[32,128,256]{2,0,1:T(8,128)S(1)} fusion(f32[32,130,256]{2,0,1:T(8,128)S(1)} %maximum_convert_fusion.1, f32[32,128,512]{2,0,1:T(8,128)} %copy-done.2), kind=kLoop, calls=%fused_computation.15 | loop fusion | flops 5242880 | bytes 25165824 | tf_op jit(solution)/shard_map/add | solution.py:158
  362.6 4.4 %copy.43 = f32[32,128,256]{2,1,0:T(8,128)} copy(f32[32,128,256]{2,0,1:T(8,128)S(1)} %fusion.8) | data formatting | bytes 8388608
  367.1 59.0 %all-reduce.5.cloned.1.call-done = (f32[256,512]{1,0:T(8,128)}, f32[512,256]{1,0:T(8,128)}, f32[256,128]{1,0:T(8,128)}) async-done(((f32[256,512]{1,0:T(8,128)}, f32[512,256]{1,0:T(8,128)}, f32[256,128]{1,0:T(8,128)}), (f32[256,512]{1,0:T(8,128)}, f32[512,256]{1,0:T(8,128)}, f32[256,128]{1,0:T(8,128)})) %all-reduce.5.cloned.1.call-update) | async-done | bytes 1179664 | tf_op jit(solution)/shard_map/psum | solution.py:13
  426.0 1.9 broadcast_multiply_fusion.1
  427.9 1.6 broadcast_multiply_fusion.2
  429.5 1.9 broadcast_multiply_fusion
  (65 shorter events, 2.1 us)
Async XLA Ops:
  7.2 89.9 %copy-start = (bf16[32,128,128]{2,1,0:T(8,128)(2,1)S(1)}, bf16[32,128,128]{2,1,0:T(8,128)(2,1)}, u32[]{:S(2)}) copy-start(bf16[32,128,128]{2,1,0:T(8,128)(2,1)} %param.12) | copy-start | bytes 3145732
  7.2 5.6 %copy-start.19 = (s32[1,1,32]{2,1,0:T(1,128)S(1)}, s32[1,1,32]{2,1,0:T(1,128)}, u32[]{:S(2)}) copy-start(s32[1,1,32]{2,1,0:T(1,128)} %param.11) | copy-start | bytes 388
  10.1 3.5 collective-permute-start
  12.7 3.5 collective-permute-start.1
  16.5 0.9 copy-start.18
  17.4 6.3 %copy-start.4 = (f32[32,128,256]{2,0,1:T(8,128)}, f32[32,128,256]{2,0,1:T(8,128)S(1)}, u32[]{:S(2)}) copy-start(f32[32,128,256]{2,0,1:T(8,128)S(1)} %get-tuple-element.24) | copy-start | bytes 12582916
  17.4 1.1 copy-start.22
  18.5 5.2 %copy-start.13 = (bf16[32,128,256]{2,0,1:T(8,128)(2,1)}, bf16[32,128,256]{2,0,1:T(8,128)(2,1)S(1)}, u32[]{:S(2)}) copy-start(bf16[32,128,256]{2,0,1:T(8,128)(2,1)S(1)} %multiply_convert_fusion.5) | copy-start | bytes 6291460
  18.5 7.1 %copy-start.6 = (bf16[32,128,256]{2,1,0:T(8,128)(2,1)S(1)}, bf16[32,128,256]{2,1,0:T(8,128)(2,1)}, u32[]{:S(2)}) copy-start(bf16[32,128,256]{2,1,0:T(8,128)(2,1)} %param.10) | copy-start | bytes 6291460
  18.5 7.1 %copy-start.15 = (bf16[512,256]{1,0:T(8,128)(2,1)S(1)}, bf16[512,256]{1,0:T(8,128)(2,1)}, u32[]{:S(2)}) copy-start(bf16[512,256]{1,0:T(8,128)(2,1)} %param.18) | copy-start | bytes 786436
  23.7 1.9 copy-start.11
  34.2 6.5 %copy-start.17 = (s32[32,128]{1,0:T(8,128)S(1)}, s32[32,128]{1,0:T(8,128)}, u32[]{:S(2)}) copy-start(s32[32,128]{1,0:T(8,128)} %param.13) | copy-start | bytes 49156
  34.2 6.5 %copy-start.20 = (s32[32]{0:T(128)S(1)}, s32[32]{0:T(128)}, u32[]{:S(2)}) copy-start(s32[32]{0:T(128)} %param.14) | copy-start | bytes 388
  34.2 62.8 %all-to-all-start = ((bf16[16,2,128,512]{3,2,1,0:T(8,128)(2,1)}), bf16[16,2,128,512]{3,2,1,0:T(8,128)(2,1)}, u32[]{:S(2)}, u32[]{:S(2)}) async-start(bf16[16,2,128,512]{3,2,1,0:T(8,128)(2,1)} %bitcast.68), calls=%async_computation | async-start | bytes 8388608 | tf_op jit(solution)/shard_map/all_to_all | solution.py:117
  99.3 4.1 copy-start.16
  99.3 4.1 copy-start.21
  102.0 1.4 copy-start.7
  105.7 1.1 copy-start.9
  110.9 3.4 copy-start.3
  127.5 5.4 %copy-start.8 = (bf16[32,256,128]{1,2,0:T(8,128)(2,1)S(1)}, bf16[32,256,128]{1,2,0:T(8,128)(2,1)}, u32[]{:S(2)}) copy-start(bf16[32,256,128]{1,2,0:T(8,128)(2,1)} %copy-done.7) | copy-start | bytes 6291460
  127.5 5.4 %copy-start.10 = (bf16[4096,128]{1,0:T(8,128)(2,1)S(1)}, bf16[4096,128]{1,0:T(8,128)(2,1)}, u32[]{:S(2)}) copy-start(bf16[4096,128]{1,0:T(8,128)(2,1)} %copy-done.9) | copy-start | bytes 3145732
  127.5 60.9 %all-to-all-start.1 = ((bf16[16,2,128,512]{3,2,1,0:T(8,128)(2,1)}), bf16[16,2,128,512]{3,2,1,0:T(8,128)(2,1)}, u32[]{:S(2)}, u32[]{:S(2)}) async-start(bf16[16,2,128,512]{3,2,1,0:T(8,128)(2,1)} %pad_maximum_fusion.1), calls=%async_computation.1 | async-start | bytes 8388608 | tf_op jit(solution)/shard_map/all_to_all | solution.py:130
  132.6 167.5 %all-reduce.7.cloned.1.call-start = ((), (), s32[]{:S(2)}) async-start(), calls=%async_computation.3 | async-start | bytes 2359296 | tf_op jit(solution)/shard_map/psum | solution.py:12
  193.8 8.8 %copy-start.2 = (f32[32,128,512]{2,0,1:T(8,128)}, f32[32,128,512]{2,0,1:T(8,128)S(1)}, u32[]{:S(2)}) copy-start(f32[32,128,512]{2,0,1:T(8,128)S(1)} %fusion.3) | copy-start | bytes 25165828
  193.8 5.2 %copy-start.12 = (bf16[32,128,512]{2,1,0:T(8,128)(2,1)S(1)}, bf16[32,128,512]{2,1,0:T(8,128)(2,1)}, u32[]{:S(2)}) copy-start(bf16[32,128,512]{2,1,0:T(8,128)(2,1)} %copy-done.11) | copy-start | bytes 12582916
  202.6 8.5 %copy-start.14 = (bf16[32,128,256]{2,0,1:T(8,128)(2,1)S(1)}, bf16[32,128,256]{2,0,1:T(8,128)(2,1)}, u32[]{:S(2)}) copy-start(bf16[32,128,256]{2,0,1:T(8,128)(2,1)} %copy-done.13) | copy-start | bytes 6291460
  209.2 2.0 copy-start.24
  211.1 4.0 copy-start.23
  214.8 211.2 %all-reduce.5.cloned.1.call-start = ((), (), s32[]{:S(2)}) async-start(), calls=%async_computation.2 | async-start | bytes 2359296 | tf_op jit(solution)/shard_map/psum | solution.py:13
  215.2 7.3 %copy-start.5 = (f32[32,128,256]{2,0,1:T(8,128)S(1)}, f32[32,128,256]{2,0,1:T(8,128)}, u32[]{:S(2)}) copy-start(f32[32,128,256]{2,0,1:T(8,128)} %copy-done.4) | copy-start | bytes 12582916
  300.1 57.2 %collective-permute-start.2 = (bf16[32,1,256]{2,0,1:T(8,128)(2,1)S(1)}, bf16[32,1,256]{2,0,1:T(8,128)(2,1)S(1)}, u32[]{:S(2)}, u32[]{:S(2)}) collective-permute-start(bf16[32,1,256]{2,0,1:T(8,128)(2,1)S(1)} %get-tuple-element.25), channel_id=1, source_target_pairs={{0,1},{1,2},{2,3},{3,4},{4,5},{5,6},{6,7},{7,8},{8,9},{9,10},{10,1... | collective-permute-start | bytes 49160 | tf_op jit(solution)/shard_map/ppermute | solution.py:23
  306.7 50.6 %collective-permute-start.3 = (bf16[32,1,256]{2,0,1:T(8,128)(2,1)S(1)}, bf16[32,1,256]{2,0,1:T(8,128)(2,1)S(1)}, u32[]{:S(2)}, u32[]{:S(2)}) collective-permute-start(bf16[32,1,256]{2,0,1:T(8,128)(2,1)S(1)} %get-tuple-element.26), channel_id=1, source_target_pairs={{1,0},{2,1},{3,2},{4,3},{5,4},{6,5},{7,6},{8,7},{9,8},{10,9},{11,1... | collective-permute-start | bytes 49160 | tf_op jit(solution)/shard_map/ppermute | solution.py:25
  357.7 73.7 %copy-start.1 = (bf16[32,128,128]{2,1,0:T(8,128)(2,1)S(1)}, bf16[32,128,128]{2,1,0:T(8,128)(2,1)}, u32[]{:S(2)}) copy-start(bf16[32,128,128]{2,1,0:T(8,128)(2,1)} %param.12) | copy-start | bytes 3145732
Sparse Core Ops, SparseCore 0:
  215.0 85.0 all-reduce.6
  302.8 123.2 all-reduce.4
